TPU v7x, 256 devices: a whole 4x4x8 slice. The times are simulated.
256 devices in a mesh: section: 2 (over x_lo), blk: 128 (over x_hi, y, z, core).
Axes of the slice: x: 4 (x_hi: 2, x_lo: 2; x = x_hi * 2 + x_lo), y: 4, z: 8, core: 2. Of those that a mesh axis runs over, the one named last changes fastest.
Arguments:
- raw_traces: bfloat16 [1024, 8192], P('blk', 'section'), may hold values from -6 to 6
- valid_mask: int32 [1024, 8], P('blk', 'section'), may hold values from 0 to 1, as said below
- block_order: int32 [128], replicated, may hold values from 0 to 127, each once
Outputs:
- correlations: float32 [16, 1024, 256], P('section', 'blk')
Inputs may be any that keep to these rules, and one draw needn't show every extreme that they name: `valid_mask`: a station either has no valid segment at all, or each of its segments is valid independently. `block_order`: each block index once.
All inputs are finite; a program needn't handle non-finite values.
Results may differ from a plain program's by a relative error of at most 0.0063.
Values may be sent and summed in bfloat16 or wider, within the bound.
A program may use at most 64 MiB of HBM per device.

v0:
```python
import math

import jax
import jax.numpy as jnp
from jax import lax
from jax.sharding import PartitionSpec as P

L = 1024
NF = 384
BIN_LO = 8
LAGS = 256
TAPS = 33
HW = 50
WF = 32
STEPS = 2
RIM = 66


def extended(x, sides, width):
    for axis, dim in sides:
        devices, length = (lax.axis_size(axis), x.shape[dim])
        up = [(i, (i + 1) % devices) for i in range(devices - 1)]
        down = [(j, i) for i, j in up]
        last = lax.slice_in_dim(x, length - width, length, axis=dim)
        initial = lax.slice_in_dim(x, 0, width, axis=dim)
        before = lax.ppermute(last, axis, up)
        after = lax.ppermute(initial, axis, down)
        x = jnp.concatenate([before, x, after], axis=dim)
    return x


def from_root(value, axis, source):
    kept = jnp.where(lax.axis_index(axis) == source, value, 0).astype(value.dtype)
    return lax.psum(kept, axis)


def bandpass_taps():
    offsets = jnp.arange(TAPS, dtype=jnp.float32) - (TAPS - 1) // 2
    low = BIN_LO / L
    high = (BIN_LO + NF) / L
    window = 0.5 + 0.5 * jnp.cos(2.0 * math.pi * offsets / (TAPS + 1))
    return window * (
        2.0 * high * jnp.sinc(2.0 * high * offsets) - 2.0 * low * jnp.sinc(2.0 * low * offsets)
    )


def filter_normalize(padded):
    taps = bandpass_taps()
    width = padded.shape[1] - (TAPS - 1)
    filtered = taps[0] * padded[:, 0:width]
    for offset in range(1, TAPS):
        filtered = filtered + taps[offset] * padded[:, offset : offset + width]
    magnitude = jnp.abs(filtered)
    window_sum = lax.reduce_window(
        magnitude, jnp.zeros((), magnitude.dtype), lax.add, (1, 2 * HW + 1), (1, 1), "VALID"
    )
    centre = filtered[:, HW : HW + window_sum.shape[1]]
    return (centre / (window_sum / (2 * HW + 1) + 1e-06)).astype(jnp.bfloat16)


def forward_table():
    times = jnp.arange(L, dtype=jnp.int32)[:, None]
    bins = BIN_LO + jnp.arange(NF, dtype=jnp.int32)[None, :]
    phase = jnp.mod(times * bins, L).astype(jnp.float32) * (2.0 * math.pi / L)
    return jnp.concatenate([jnp.cos(phase), -jnp.sin(phase)], axis=1).astype(jnp.bfloat16)


def lag_table():
    bins = BIN_LO + jnp.arange(NF, dtype=jnp.int32)[:, None]
    shifts = jnp.arange(LAGS, dtype=jnp.int32)[None, :] - LAGS // 2
    phase = jnp.mod(bins * shifts, L).astype(jnp.float32) * (2.0 * math.pi / L)
    scale = 1.0 / math.sqrt(NF)
    return jnp.concatenate([jnp.cos(phase) * scale, -jnp.sin(phase) * scale], axis=0)


def whiten(normalized, maskvals):
    stations = normalized.shape[0]
    framed = normalized.reshape(-1, L)
    spectra = jnp.dot(framed, forward_table(), preferred_element_type=jnp.float32)
    spectra = spectra.reshape(stations, -1, 2 * NF)
    real_part = spectra[:, :, :NF]
    imag_part = spectra[:, :, NF:]
    amplitude = jnp.sqrt(real_part * real_part + imag_part * imag_part)
    smooth = lax.reduce_window(
        amplitude,
        jnp.zeros((), amplitude.dtype),
        lax.add,
        (1, 1, 2 * WF + 1),
        (1, 1, 1),
        ((0, 0), (0, 0), (WF, WF)),
    )
    factor = maskvals[:, :, None] / (smooth / (2 * WF + 1) + 1e-06)
    return jnp.concatenate([real_part * factor, imag_part * factor], axis=2).astype(jnp.bfloat16)


def cross_lags(sources, receivers):
    source_real = sources[:, :, :NF]
    source_imag = sources[:, :, NF:]
    recv_real = receivers[:, :, :NF]
    recv_imag = receivers[:, :, NF:]
    real_sum = jnp.einsum(
        "jsf,isf->jif", source_real, recv_real, preferred_element_type=jnp.float32
    ) + jnp.einsum("jsf,isf->jif", source_imag, recv_imag, preferred_element_type=jnp.float32)
    imag_sum = jnp.einsum(
        "jsf,isf->jif", source_real, recv_imag, preferred_element_type=jnp.float32
    ) - jnp.einsum("jsf,isf->jif", source_imag, recv_real, preferred_element_type=jnp.float32)
    stacked = jnp.concatenate([real_sum, imag_sum], axis=2)
    count_src, count_rec = (stacked.shape[0], stacked.shape[1])
    lagged = jnp.dot(
        stacked.reshape(count_src * count_rec, 2 * NF), lag_table(), precision=lax.Precision.HIGHEST
    )
    return lagged.reshape(count_src, count_rec, LAGS)


def shards(raw_traces, valid_mask, block_order):
    padded = extended(raw_traces, (("section", 1),), RIM)
    normalized = filter_normalize(padded.astype(jnp.float32))
    maskvals = valid_mask.astype(jnp.float32)
    whitened = whiten(normalized, maskvals)
    mask_wire = valid_mask.astype(jnp.bfloat16)
    stations = whitened.shape[0]
    source_parts = []
    source_masks = []
    for position in range(STEPS):
        block_spec, block_mask = (
            from_root(whitened, "blk", block_order[position]),
            from_root(mask_wire, "blk", block_order[position]),
        )
        source_parts.append(block_spec)
        source_masks.append(block_mask)
    sources = jnp.concatenate(source_parts, axis=0)
    source_mask = jnp.concatenate(source_masks, axis=0).astype(jnp.float32)
    half_count = sources.shape[0] // 2
    section_index = lax.axis_index("section")
    partial_counts = jnp.dot(source_mask, maskvals.T, precision=lax.Precision.HIGHEST)
    counts = lax.psum(partial_counts, "section")
    start = jnp.int32(0)

    def one_block(offset):
        block_spec = lax.dynamic_slice_in_dim(sources, start + offset * stations, stations, 0)
        return cross_lags(block_spec, whitened)

    lagged = lax.map(
        one_block, jnp.arange(half_count * lax.axis_size("section") // stations, dtype=jnp.int32)
    )
    summed_lags = lax.psum_scatter(
        lagged.reshape(half_count * lax.axis_size("section"), stations, LAGS),
        "section",
        scatter_dimension=0,
        tiled=True,
    )
    own_counts = lax.dynamic_slice_in_dim(counts, section_index * half_count, half_count, 0)
    return summed_lags / jnp.maximum(own_counts, 1.0)[:, :, None]


def solution(mesh):
    return jax.shard_map(
        shards,
        mesh=mesh,
        in_specs=(P("blk", "section"), P("blk", "section"), P()),
        out_specs=P("section", "blk", None),
        check_vma=False,
    )
```

profile of v0, /device:TPU:1, one launch (start us, length us, event | category | flops | bytes accessed | tf_op | source)
XLA Modules:
  0.0 1282.6 jit_solution(17670595992251923281)
XLA Ops:
  6.5 0.0 all-reduce.3.cloned.1.call-start
  6.5 0.8 fusion.72
  7.4 3.9 collective-permute-start
  11.3 1.3 collective-permute-start.1
  12.6 0.1 fusion.65
  12.7 0.7 fusion.74
  13.4 6.5 cosine_convert_fusion
  19.9 0.0 copy-done.2
  19.9 0.6 fusion.73
  21.8 0.0 copy-done.1
  21.8 0.6 broadcast_select_fusion.3
  22.4 0.7 fusion.75
  23.1 0.0 collective-permute-done
  23.1 0.0 collective-permute-done.1
  23.1 0.1 concatenate.29
  23.2 21.8 %fusion.69 = (f32[8,4196]{1,0:T(8,128)S(1)}, f32[8,4196]{1,0:T(8,128)S(1)}) fusion(f32[8,4228]{1,0:T(8,128)S(1)} %convert_element_type.37, f32[]{:T(128)} %bitcast.38, f32[]{:T(128)} %bitcast.37, f32[]{:T(128)} %bitcast.36, f32[]{:T(128)} %bitcast.35, f32[]{:T(128)} %bitcast.34, f32[]{:T(128)} %bitcast.33, f32[]{:T(128)} %bitcast.32, f32[]{:T(128)} %bitcast.31, ...), kind=kLoop, calls=%fused_computation.155 | loop fusion | flops 2215488 | bytes 4699652 | tf_op jit(solution)/shard_map/abs | solution.py:53
  45.0 65.2 %reduce_window.14 = f32[8,4096]{1,0:T(8,128)S(1)} reduce-window(f32[8,4196]{1,0:T(8,128)S(1)} %get-tuple-element.93, f32[]{:T(128)} %constant.132.clone.1), window={size=1x101}, to_apply=%region_0.2 | reduce-window | flops 3276800 | bytes 265348 | tf_op jit(solution)/shard_map/reduce_window | solution.py:54
  110.2 0.1 fusion.49
  110.3 0.4 fusion.15
  110.7 12.9 %reduce_window.15 = f32[8,4,384]{2,0,1:T(8,128)S(1)} reduce-window(f32[8,4,384]{2,0,1:T(8,128)S(1)} %add_sqrt_fusion, f32[]{:T(128)} %constant.132.clone.1), window={size=1x1x65 pad=0_0x0_0x32_32}, to_apply=%region_1.3 | reduce-window | flops 786432 | bytes 98308 | tf_op jit(solution)/shard_map/reduce_window | solution.py:84
  123.6 0.1 multiply_convert_fusion.1
  123.7 0.6 pad_maximum_fusion.1
  124.3 0.0 all-reduce.3.cloned.1.call-update
  124.4 0.0 reduce-scatter.2.cloned.1.call-start
  124.5 1116.5 %all-reduce.3.cloned.1.call-done = (bf16[8,4,768]{2,0,1:T(8,128)(2,1)}, bf16[8,4,768]{2,0,1:T(8,128)(2,1)}, bf16[8,4]{0,1:T(4,128)(2,1)}, bf16[8,4]{0,1:T(4,128)(2,1)}) async-done(((bf16[8,4,768]{2,0,1:T(8,128)(2,1)}, bf16[8,4,768]{2,0,1:T(8,128)(2,1)}, bf16[8,4]{0,1:T(4,128)(2,1)}, bf16[8,4]{0,1:T(4,128)(2,1)}), (bf16[8,4,768]{2,0,1:T(8,128)(2,1)}, bf16[8,4,768]{2,0,1:T(8,128)(2,1)}, ...) | async-done | bytes 98448 | tf_op jit(solution)/shard_map/psum | solution.py:34
  1241.0 0.8 pad_maximum_fusion
  1241.8 0.0 copy-start.3
  1241.8 0.0 copy-start.4
  1241.9 19.7 %while.12 = (s32[]{:T(128)}, f32[2,8,8,256]{3,2,1,0:T(8,128)}, s32[2]{0:T(128)S(1)}, bf16[16,4,768]{2,0,1:T(8,128)(2,1)S(1)}, bf16[8,4,768]{2,1,0:T(4,128)(2,1)S...) while((s32[]{:T(128)}, f32[2,8,8,256]{3,2,1,0:T(8,128)}, s32[2]{0:T(128)S(1)}, ...), condition=%wide.region_5.7_spmd, body=%wide.region_4.6_spmd.sunk | while | flops 153748096 | bytes 4200115 | solution.py:143
  1241.9 0.6 dynamic_slice.19
  1243.1 0.2 copy.27
  1243.4 0.3 copy.28
  1243.7 0.6 fusion.114
  1244.3 0.5 copy.29
  1244.8 0.3 copy.30
  1245.1 0.3 copy.31
  1245.4 0.6 fusion.115
  1246.0 0.5 copy.32
  1246.5 0.7 fusion.116
  1247.2 0.5 copy.33
  1247.7 0.7 fusion.117
  1248.4 0.5 copy.34
  1249.0 1.6 cosine_multiply_fusion.2
  1250.6 1.1 fusion.118
  1251.7 0.6 dynamic_slice.19
  1253.0 0.2 copy.27
  1253.3 0.3 copy.28
  1253.5 0.6 fusion.114
  1254.2 0.5 copy.29
  1254.7 0.3 copy.30
  1255.0 0.3 copy.31
  1255.2 0.6 fusion.115
  1255.9 0.5 copy.32
  1256.4 0.7 fusion.116
  1257.1 0.5 copy.33
  1257.6 0.7 fusion.117
  1258.2 0.5 copy.34
  1258.8 1.6 cosine_multiply_fusion.2
  1260.4 1.2 fusion.118
  1261.6 0.0 reduce-scatter.2.cloned.1.call-update
  1261.6 0.3 fusion.50
  1261.9 3.8 psum.39
  1265.7 8.3 reduce-scatter.2.cloned.1.call-done
  1274.0 1.5 broadcast_divide_fusion
  (24 shorter events, 0.2 us)
Async XLA Ops:
  6.5 16.6 %copy-start = (bf16[8,4096]{1,0:T(8,128)(2,1)S(1)}, bf16[8,4096]{1,0:T(8,128)(2,1)}, u32[]{:S(2)}) copy-start(bf16[8,4096]{1,0:T(8,128)(2,1)} %param.6) | copy-start | bytes 196612
  6.5 13.4 %copy-start.2 = (s32[128]{0:T(128)S(1)}, s32[128]{0:T(128)}, u32[]{:S(2)}) copy-start(s32[128]{0:T(128)} %param.8) | copy-start | bytes 1540
  6.5 15.2 %copy-start.1 = (s32[8,4]{0,1:T(4,128)S(1)}, s32[8,4]{0,1:T(4,128)}, u32[]{:S(2)}) copy-start(s32[8,4]{0,1:T(4,128)} %param.7) | copy-start | bytes 388
  6.5 1234.5 %all-reduce.3.cloned.1.call-start = ((), (), s32[]{:S(2)}) async-start(), calls=%async_computation.2 | async-start | bytes 200704 | tf_op jit(solution)/shard_map/psum | solution.py:34
  7.4 15.7 %collective-permute-start = (bf16[8,66]{1,0:T(8,128)(2,1)S(1)}, bf16[8,66]{1,0:T(8,128)(2,1)S(1)}, u32[]{:S(2)}, u32[]{:S(2)}) collective-permute-start(bf16[8,66]{1,0:T(8,128)(2,1)S(1)} %get-tuple-element.106), channel_id=1, source_target_pairs={{0,128},{1,129},{2,130},{3,131},{4,132},{5,133},{6,134},{7,135},{8... | collective-permute-start | bytes 3176 | tf_op jit(solution)/shard_map/ppermute | solution.py:26
  11.3 11.8 collective-permute-start.1
  124.4 1149.7 %reduce-scatter.2.cloned.1.call-start = ((), (), s32[]{:S(2)}) async-start(), calls=%async_computation.1 | async-start | bytes 196608 | tf_op jit(solution)/shard_map/reduce_scatter | solution.py:146
  1241.8 19.8 %copy-start.3 = (bf16[8,4]{0,1:T(4,128)(2,1)S(1)}, bf16[8,4]{0,1:T(4,128)(2,1)}, u32[]{:S(2)}) copy-start(bf16[8,4]{0,1:T(4,128)(2,1)} %get-tuple-element.91) | copy-start | bytes 196
  1241.8 19.8 %copy-start.4 = (bf16[8,4]{0,1:T(4,128)(2,1)S(1)}, bf16[8,4]{0,1:T(4,128)(2,1)}, u32[]{:S(2)}) copy-start(bf16[8,4]{0,1:T(4,128)(2,1)} %get-tuple-element.92) | copy-start | bytes 196
Sparse Core Ops, SparseCore 0:
  124.5 1116.4 all-reduce.2
  1261.7 12.2 reduce-scatter.1
where the time goes:
time: 1290 us; the launch traced here: 1280 us
  waiting for transfers between devices  1120 us (87%)
  other arithmetic  114 us (9%)
  between operations  15.1 us (1%)
    psum x1, waiting for transfers between devices, from_root(): return lax.psum(kept, axis)  1120 us
    another operation x1, other arithmetic, filter_normalize(): lax.reduce_window(magnitude, jnp.zeros((), magnitude.dtype), lax.add, (1,...  65.2 us
  transfers between devices with their start and end apart: 4, of which 2 were waited for; matrix products, arithmetic and copies ran while one was open for 1% of the time, Pallas kernels for 0%

commit v1 on v0

v1 whole, which is shorter than its diff:
```python
import functools
import math

import jax
import jax.numpy as jnp
import ml_dtypes
import numpy as np
from jax import lax
from jax.experimental import pallas as pl
from jax.experimental.pallas import tpu as pltpu
from jax.sharding import PartitionSpec as P

L = 1024
NF = 384
BIN_LO = 8
LAGS = 256
TAPS = 33
HW = 50
WF = 32
NT = 32
KT = NF // 128
SEG = 4
ST = 8
PIECES = SEG * KT + 1
PLANE = 16
DEPTH = 8
MESH = pl.DeviceIdType.MESH
f32 = jnp.float32
bf16 = jnp.bfloat16


def split(values):
    high = values.astype(np.float32).astype(ml_dtypes.bfloat16)
    low = (values - high.astype(np.float64)).astype(ml_dtypes.bfloat16)
    return high, low


def tables():
    half = (TAPS - 1) // 2
    k = np.arange(-half, half + 1).astype(np.float64)
    a, b = BIN_LO / L, (BIN_LO + NF) / L
    taps = (0.5 + 0.5 * np.cos(2 * np.pi * k / (TAPS + 1))) * (
        2 * b * np.sinc(2 * b * k) - 2 * a * np.sinc(2 * a * k)
    )
    shift = np.arange(128)[None, :] + 128 - np.arange(384)[:, None]
    band = np.where(np.abs(shift) <= half, taps[np.clip(shift + half, 0, TAPS - 1)], 0.0)
    fir = np.concatenate(split(band), axis=1)
    box = (np.abs(shift) <= HW).astype(ml_dtypes.bfloat16)
    box = np.concatenate([box, box], axis=0)
    bins = BIN_LO + np.arange(NF)
    phase = (np.arange(L)[:, None] * bins[None, :]) % L * (2 * np.pi / L)
    dft = np.concatenate([np.cos(phase), -np.sin(phase)], axis=1)
    dft = dft.astype(np.float32).astype(ml_dtypes.bfloat16)
    near = np.abs(np.arange(NF)[:, None] - np.arange(NF)[None, :]) <= WF
    near = near.astype(ml_dtypes.bfloat16)
    phase = (bins[:, None] * (np.arange(LAGS) - LAGS // 2)[None, :]) % L * (2 * np.pi / L)
    lag = np.concatenate([np.cos(phase), -np.sin(phase)], axis=0) / math.sqrt(NF)
    lag = np.concatenate(split(lag), axis=1)
    return fir, box, dft, near, lag


def dot(a, b):
    return jnp.dot(a, b, preferred_element_type=f32)


def halves(x):
    high = x.astype(bf16)
    return high, (x - high.astype(f32)).astype(bf16)


def normalize(tiles, fir, box):
    zero = jnp.zeros((ST, 128), f32)
    left = jnp.concatenate([zero] + tiles[:-1], axis=0).astype(bf16)
    mid = jnp.concatenate(tiles, axis=0).astype(bf16)
    right = jnp.concatenate(tiles[1:] + [zero], axis=0).astype(bf16)
    both = dot(jnp.concatenate([left, mid, right], axis=1), fir)
    filtered = both[:, :128] + both[:, 128:]
    size = jnp.abs(filtered)
    rows = NT * ST
    parts = [halves(size[ST * i : ST * i + rows]) for i in range(3)]
    window = dot(jnp.concatenate([p[0] for p in parts] + [p[1] for p in parts], axis=1), box)
    return filtered[ST : ST + rows] / (window * (1.0 / (2 * HW + 1)) + 1e-06)


def spectra_of(normalized, dft, near, mask):
    per = L // 128
    lanes = [
        jnp.concatenate(
            [normalized[(g * per + t) * ST : (g * per + t + 1) * ST] for g in range(SEG)], axis=0
        )
        for t in range(per)
    ]
    spectra = dot(jnp.concatenate(lanes, axis=1).astype(bf16), dft)
    re, im = spectra[:, :NF], spectra[:, NF:]
    high, low = halves(jnp.sqrt(re * re + im * im))
    smooth = dot(high, near) + dot(low, near)
    factor = mask / (smooth * (1.0 / (2 * WF + 1)) + 1e-06)
    return re * factor, im * factor


def kernel(
    raw_ref, mask_ref, order_ref, fir_hbm, box_hbm, dft_hbm, near_hbm, lag_hbm, out_ref,
    fir_ref, box_ref, dft_ref, near_ref, lag_ref,
    halo, wfull, slots1, cand, slots2, picked, slots3, stack,
    table_sem, halo_sem, pair_sem, one_sem, two_sem, three_sem,
):
    half = lax.axis_index("section")
    blk = lax.axis_index("blk")
    me = (blk // 16) * 2 + blk % 2
    z = (blk // 2) % DEPTH
    collects = me < PIECES

    def device(section, plane, depth):
        return (section, (plane // 2) * 16 + depth * 2 + plane % 2)

    def remote(src, dst, sems, to):
        return pltpu.make_async_remote_copy(
            src_ref=src, dst_ref=dst, send_sem=sems.at[0], recv_sem=sems.at[1],
            device_id=to, device_id_type=MESH,
        )

    def wait(ref, sem):
        pltpu.make_async_copy(ref, ref, sem).wait()

    copies = [
        pltpu.make_async_copy(src, dst, table_sem.at[i])
        for i, (src, dst) in enumerate(
            (
                (fir_hbm, fir_ref), (box_hbm, box_ref), (dft_hbm, dft_ref),
                (near_hbm, near_ref), (lag_hbm, lag_ref),
            )
        )
    ]
    for copy in copies:
        copy.start()

    mates = [lax.rem(me + i, PLANE) for i in range(1, PLANE)]
    column = [(i // DEPTH, i % DEPTH) for i in range(1, 2 * DEPTH)]
    column = [(lax.rem(half + i, 2), lax.rem(z + j, DEPTH)) for i, j in column]

    barrier = pltpu.get_barrier_semaphore()
    for mate in mates:
        pl.semaphore_signal(barrier, inc=1, device_id=device(half, mate, z), device_id_type=MESH)
    for section, depth in column:
        pl.semaphore_signal(
            barrier, inc=1, device_id=device(section, me, depth), device_id_type=MESH
        )
    pl.semaphore_wait(barrier, len(mates) + len(column))

    other = device(1 - half, me, z)
    edge = pl.multiple_of((1 - half) * ((NT - 1) * 128), 128)
    send_halo = remote(raw_ref.at[:, pl.ds(edge, 128)], halo, halo_sem, other)
    send_halo.start()
    raw = raw_ref[...].astype(f32)
    send_halo.wait()
    beyond = halo[...].astype(f32)
    tiles = [raw[:, 128 * i : 128 * (i + 1)] for i in range(NT)]
    before = jnp.where(half == 1, beyond, 0.0)
    after = jnp.where(half == 0, beyond, 0.0)
    copies[0].wait()
    copies[1].wait()
    normalized = normalize([before] + tiles + [after], fir_ref[...], box_ref[...])
    mask = mask_ref[...].astype(f32)
    column_mask = jnp.concatenate([mask[:, g : g + 1] for g in range(SEG)], axis=0)
    copies[2].wait()
    copies[3].wait()
    re, im = spectra_of(normalized, dft_ref[...], near_ref[...], column_mask)
    for g in range(SEG):
        for k in range(KT):
            place = (slice(ST * g, ST * (g + 1)), slice(128 * k, 128 * (k + 1)))
            piece = jnp.concatenate([re[place], im[place]], axis=0)
            wfull[half, g * KT + k] = piece.astype(bf16)
    lane = lax.broadcasted_iota(jnp.int32, (ST, 128), 1)
    flags = jnp.zeros((ST, 128), f32)
    for g in range(SEG):
        flags = jnp.where(lane == g, mask[:, g : g + 1], flags)
    wfull[half, PIECES - 1] = jnp.concatenate([flags, flags], axis=0).astype(bf16)

    for mate in mates:

        @pl.when(mate < PIECES)
        def _(mate=mate):
            remote(
                wfull.at[half, mate], slots1.at[me], one_sem, device(half, mate, z)
            ).start()

    pair = remote(wfull.at[half], wfull.at[half], pair_sem, other)
    pair.start()

    root = [order_ref[i] for i in range(2)]
    root_plane = [(r // 16) * 2 + r % 2 for r in root]
    mine = jnp.where(half == 0, root[0], root[1])
    mine_z = (mine // 2) % DEPTH

    @pl.when(collects)
    def _():
        slots1[me] = wfull[half, me]
        wait(slots1.at[pl.ds(0, PLANE - 1)], one_sem.at[1])
        for i in range(2):
            cand[i] = slots1[root_plane[i]]
        for section, depth in column:
            remote(
                cand.at[section], slots2.at[half, z], two_sem, device(section, me, depth)
            ).start()
        slots2[half, z] = cand[half]
        wait(slots1.at[pl.ds(0, PLANE - 1)], two_sem.at[1])
        for i in range(2):
            picked[i] = slots2[i, mine_z]
        for mate in mates:
            remote(picked, slots3.at[me], three_sem, device(half, mate, z)).start()
        for i in range(2):
            slots3[me, i] = picked[i]

    pair.wait()
    copies[4].wait()

    @pl.when(collects)
    def _():
        wait(slots3.at[pl.ds(0, PIECES - 1)], three_sem.at[1])

    @pl.when(jnp.logical_not(collects))
    def _():
        wait(slots3.at[pl.ds(0, PIECES)], three_sem.at[1])

    for k in range(KT):
        real = [jnp.zeros((ST, 128), f32)] * ST
        imag = [jnp.zeros((ST, 128), f32)] * ST
        for i in range(2):
            for g in range(SEG):
                station = wfull[i, g * KT + k].astype(f32)
                source = slots3[g * KT + k, i].astype(f32)
                re_s, im_s = station[:ST], station[ST:]
                for n in range(ST):
                    re_n = source[n : n + 1]
                    im_n = source[ST + n : ST + n + 1]
                    real[n] = real[n] + (re_s * re_n + im_s * im_n)
                    imag[n] = imag[n] + (im_s * re_n - re_s * im_n)
        for n in range(ST):
            stack[ST * n : ST * (n + 1), 128 * k : 128 * (k + 1)] = real[n]
            stack[ST * n : ST * (n + 1), NF + 128 * k : NF + 128 * (k + 1)] = imag[n]
    high, low = halves(stack[...])
    first = dot(high, lag_ref[...])
    lagged = first[:, :LAGS] + first[:, LAGS:] + dot(low, lag_ref[:, :LAGS])
    own = [wfull[i, PIECES - 1].astype(f32)[:ST] for i in range(2)]
    theirs = [slots3[PIECES - 1, i].astype(f32)[:ST] for i in range(2)]
    for n in range(ST):
        count = own[0] * theirs[0][n : n + 1] + own[1] * theirs[1][n : n + 1]
        count = jnp.maximum(jnp.sum(count, axis=1, keepdims=True), 1.0)
        out_ref[n] = lagged[ST * n : ST * (n + 1)] / count

    @pl.when(jnp.logical_not(collects))
    def _():
        wait(slots1.at[pl.ds(0, PIECES)], one_sem.at[0])

    @pl.when(collects)
    def _():
        wait(slots1.at[pl.ds(0, PIECES - 1)], one_sem.at[0])
        wait(slots1.at[pl.ds(0, PLANE - 1)], two_sem.at[0])
        wait(slots3.at[pl.ds(0, PLANE - 1)], three_sem.at[0])


def shards(raw_traces, valid_mask, block_order):
    constants = [jnp.asarray(t) for t in tables()]
    vmem = pl.BlockSpec(memory_space=pltpu.VMEM)
    piece = (2 * ST, 128)
    pair = pltpu.SemaphoreType.DMA((2,))
    return pl.pallas_call(
        kernel,
        out_shape=jax.ShapeDtypeStruct((ST, ST, LAGS), f32),
        in_specs=[vmem, vmem, pl.BlockSpec(memory_space=pltpu.SMEM)]
        + [pl.BlockSpec(memory_space=pl.ANY)] * len(constants),
        out_specs=vmem,
        scratch_shapes=[pltpu.VMEM(c.shape, c.dtype) for c in constants]
        + [
            pltpu.VMEM((ST, 128), bf16),
            pltpu.VMEM((2, PIECES) + piece, bf16),
            pltpu.VMEM((PLANE,) + piece, bf16),
            pltpu.VMEM((2,) + piece, bf16),
            pltpu.VMEM((2, DEPTH) + piece, bf16),
            pltpu.VMEM((2,) + piece, bf16),
            pltpu.VMEM((PLANE, 2) + piece, bf16),
            pltpu.VMEM((ST * ST, 2 * NF), f32),
            pltpu.SemaphoreType.DMA((len(constants),)),
            pair, pair, pair, pair, pair,
        ],
        compiler_params=pltpu.CompilerParams(
            collective_id=0, has_side_effects=True, vmem_limit_bytes=48 << 20
        ),
    )(raw_traces, valid_mask, block_order, *constants)


def solution(mesh):
    return jax.shard_map(
        shards,
        mesh=mesh,
        in_specs=(P("blk", "section"), P("blk", "section"), P()),
        out_specs=P("section", "blk", None),
        check_vma=False,
    )
```

time: 1290 us -> 40.8 us (0.03)
  waiting for transfers between devices: 1120 us -> 0 us
  other arithmetic: 114 us -> 0 us
  Pallas kernels: 0 us -> 32.2 us
  between operations: 15.1 us -> 0.02 us
    psum x1 -> x0, waiting for transfers between devices: 1120 us -> none  [from_root(): return lax.psum(kept, axis)]
    another operation x4 -> x0, other arithmetic: 84.6 us -> none  [the longest x1 65.2 us: filter_normalize(): lax.reduce_window(magnitude, jnp.zeros((), magnitude.dtype), lax.add, (1,...]
    pallas_call x0 -> x1, Pallas kernels: none -> 32.2 us  [shards(): pl.pallas_call(kernel, out_shape=jax.ShapeDtypeStruct((ST, ST, LAGS), f32...]
    abs x1 -> x0, other arithmetic: 21.8 us -> none  [filter_normalize(): magnitude = jnp.abs(filtered)]
  transfers between devices with their start and end apart: 4 -> 0, of which waited for: 2 -> 0; matrix products, arithmetic and copies ran while one was open for 1% -> 0% of each run, Pallas kernels for 0% -> 0%
where the time goes in v1:
time: 40.8 us; the launch traced here: 40.5 us
  Pallas kernels  32.2 us (79%)
  local copies, waits for them, and re-layouts  8.23 us (20%)
    pallas_call x1, Pallas kernels, shards(): pl.pallas_call(kernel, out_shape=jax.ShapeDtypeStruct((ST, ST, LAGS), f32...  32.2 us
    unnamed x16, local copies, waits for them, and re-layouts  8.23 us

profile of v1, /device:TPU:1, one launch (start us, length us, event | category | flops | bytes accessed | tf_op | source)
XLA Modules:
  0.0 40.5 jit_solution(8397164607902197467)
XLA Ops:
  0.0 0.8 %copy.9.mask_ref = s32[8,4]{1,0:T(8,128)S(1)} copy(s32[8,4]{0,1:T(4,128)} %param.9) | data formatting | bytes 256 | tf_op args[1]
  0.8 0.0 copy-start
  0.8 1.4 %copy-done = bf16[1024,768]{1,0:T(8,128)(2,1)S(1)} copy-done((bf16[1024,768]{1,0:T(8,128)(2,1)S(1)}, bf16[1024,768]{1,0:T(8,128)(2,1)}, u32[]{:S(2)}) %copy-start) | copy-done | bytes 1572888
  2.2 0.0 copy-start.1
  2.2 1.1 %copy-done.1 = bf16[768,512]{1,0:T(8,128)(2,1)S(1)} copy-done((bf16[768,512]{1,0:T(8,128)(2,1)S(1)}, bf16[768,512]{1,0:T(8,128)(2,1)}, u32[]{:S(2)}) %copy-start.1) | copy-done | bytes 786456
  3.3 0.0 copy-start.2
  3.3 1.0 %copy-done.2 = bf16[384,384]{1,0:T(8,128)(2,1)S(1)} copy-done((bf16[384,384]{1,0:T(8,128)(2,1)S(1)}, bf16[384,384]{1,0:T(8,128)(2,1)}, u32[]{:S(2)}) %copy-start.2) | copy-done | bytes 294936
  4.3 0.0 copy-start.3
  4.3 0.9 %copy-done.3 = bf16[768,128]{1,0:T(8,128)(2,1)S(1)} copy-done((bf16[768,128]{1,0:T(8,128)(2,1)S(1)}, bf16[768,128]{1,0:T(8,128)(2,1)}, u32[]{:S(2)}) %copy-start.3) | copy-done | bytes 196632
  5.2 0.0 copy-start.4
  5.2 0.9 %copy-done.4 = bf16[384,256]{1,0:T(8,128)(2,1)S(1)} copy-done((bf16[384,256]{1,0:T(8,128)(2,1)S(1)}, bf16[384,256]{1,0:T(8,128)(2,1)}, u32[]{:S(2)}) %copy-start.4) | copy-done | bytes 196632
  6.1 0.0 copy-start.5
  6.1 0.8 %copy-done.5 = bf16[8,4096]{1,0:T(8,128)(2,1)S(1)} copy-done((bf16[8,4096]{1,0:T(8,128)(2,1)S(1)}, bf16[8,4096]{1,0:T(8,128)(2,1)}, u32[]{:S(2)}) %copy-start.5) | copy-done | bytes 65560
  7.0 0.0 copy-start.6
  7.0 0.7 %copy-done.6 = s32[128]{0:T(128)S(1)} copy-done((s32[128]{0:T(128)S(1)}, s32[128]{0:T(128)}, u32[]{:S(2)}) %copy-start.6) | copy-done | bytes 536
  7.6 32.2 %shard_map.82 = f32[8,8,256]{2,1,0:T(8,128)S(1)} custom-call(bf16[8,4096]{1,0:T(8,128)(2,1)S(1)} %copy-done.5, s32[8,4]{1,0:T(8,128)S(1)} %copy.9.mask_ref, s32[128]{0:T(128)S(1)} %copy-done.6, bf16[384,256]{1,0:T(8,128)(2,1)S(1)} %copy-done.4, bf16[768,128]{1,0:T(8,128)(2,1)S(1)} %copy-done.3, bf16[1024,768]{1,0:T(8,128)(2,1)S(1)} %copy-done, ...), custom_call_target="tpu_custom_call" | custom-call | tf_op jit(solution)/shard_map/pallas_call | solution.py:267
  39.9 0.6 %copy.11 = f32[8,8,256]{2,1,0:T(8,128)} copy(f32[8,8,256]{2,1,0:T(8,128)S(1)} %shard_map.82) | data formatting | bytes 131072
Async XLA Ops:
  0.8 1.4 %copy-start = (bf16[1024,768]{1,0:T(8,128)(2,1)S(1)}, bf16[1024,768]{1,0:T(8,128)(2,1)}, u32[]{:S(2)}) copy-start(bf16[1024,768]{1,0:T(8,128)(2,1)} %constant.12.clone.dft_hbm) | copy-start | bytes 4718596
  2.2 1.1 %copy-start.1 = (bf16[768,512]{1,0:T(8,128)(2,1)S(1)}, bf16[768,512]{1,0:T(8,128)(2,1)}, u32[]{:S(2)}) copy-start(bf16[768,512]{1,0:T(8,128)(2,1)} %constant.14.clone.lag_hbm) | copy-start | bytes 2359300
  3.3 1.0 %copy-start.2 = (bf16[384,384]{1,0:T(8,128)(2,1)S(1)}, bf16[384,384]{1,0:T(8,128)(2,1)}, u32[]{:S(2)}) copy-start(bf16[384,384]{1,0:T(8,128)(2,1)} %constant.13.clone.near_hbm) | copy-start | bytes 884740
  4.3 0.9 %copy-start.3 = (bf16[768,128]{1,0:T(8,128)(2,1)S(1)}, bf16[768,128]{1,0:T(8,128)(2,1)}, u32[]{:S(2)}) copy-start(bf16[768,128]{1,0:T(8,128)(2,1)} %constant.11.clone.box_hbm) | copy-start | bytes 589828
  5.2 0.9 %copy-start.4 = (bf16[384,256]{1,0:T(8,128)(2,1)S(1)}, bf16[384,256]{1,0:T(8,128)(2,1)}, u32[]{:S(2)}) copy-start(bf16[384,256]{1,0:T(8,128)(2,1)} %constant.10.clone.fir_hbm) | copy-start | bytes 589828
  6.1 0.8 %copy-start.5 = (bf16[8,4096]{1,0:T(8,128)(2,1)S(1)}, bf16[8,4096]{1,0:T(8,128)(2,1)}, u32[]{:S(2)}) copy-start(bf16[8,4096]{1,0:T(8,128)(2,1)} %raw_ref.1) | copy-start | bytes 196612
  7.0 0.7 %copy-start.6 = (s32[128]{0:T(128)S(1)}, s32[128]{0:T(128)}, u32[]{:S(2)}) copy-start(s32[128]{0:T(128)} %order_ref.1) | copy-start | bytes 1540

commit v2 on v1

v2 whole, which is shorter than its diff:
```python
import math

import jax
import jax.numpy as jnp
import ml_dtypes
import numpy as np
from jax import lax
from jax.experimental import pallas as pl
from jax.experimental.pallas import tpu as pltpu
from jax.sharding import PartitionSpec as P

L = 1024
NF = 384
BIN_LO = 8
LAGS = 256
TAPS = 33
HW = 50
WF = 32
KT = NF // 128
SEGS = 8
SEG = 4
HALF = SEG * L
ST = 8
PIECE = 256
VMEM_KIB = 61920
PLANE = 16
DEPTH = 8
MESH = pl.DeviceIdType.MESH
f32 = jnp.float32
bf16 = jnp.bfloat16


def split(values):
    high = values.astype(np.float32).astype(ml_dtypes.bfloat16)
    low = (values - high.astype(np.float64)).astype(ml_dtypes.bfloat16)
    return high, low


def tables():
    half = (TAPS - 1) // 2
    k = np.arange(-half, half + 1).astype(np.float64)
    a, b = BIN_LO / L, (BIN_LO + NF) / L
    taps = (0.5 + 0.5 * np.cos(2 * np.pi * k / (TAPS + 1))) * (
        2 * b * np.sinc(2 * b * k) - 2 * a * np.sinc(2 * a * k)
    )
    shift = np.arange(128)[None, :] + 128 - np.arange(384)[:, None]
    band = np.where(np.abs(shift) <= half, taps[np.clip(shift + half, 0, TAPS - 1)], 0.0)
    fir = np.concatenate(split(band), axis=1)
    box = (np.abs(shift) <= HW).astype(ml_dtypes.bfloat16)
    box = np.concatenate([box, box], axis=0)
    bins = BIN_LO + np.arange(NF)
    phase = (np.arange(L)[:, None] * bins[None, :]) % L * (2 * np.pi / L)
    dft = np.concatenate([np.cos(phase), -np.sin(phase)], axis=1)
    dft = dft.astype(np.float32).astype(ml_dtypes.bfloat16)
    near = np.abs(np.arange(NF)[:, None] - np.arange(NF)[None, :]) <= WF
    near = near.astype(ml_dtypes.bfloat16)
    phase = (bins[:, None] * (np.arange(LAGS) - LAGS // 2)[None, :]) % L * (2 * np.pi / L)
    lag = np.concatenate([np.cos(phase), -np.sin(phase)], axis=0) / math.sqrt(NF)
    lag = np.concatenate(split(lag), axis=1)
    return fir, box, dft, near, lag


def dot(a, b):
    return jnp.dot(a, b, preferred_element_type=f32)


def halves(x):
    high = x.astype(bf16)
    return high, (x - high.astype(f32)).astype(bf16)


def whiten(tiles, masks, fir, box, dft, near):
    count = len(tiles)
    zero = jnp.zeros((ST, 128), f32)
    left = jnp.concatenate([zero, zero] + tiles, axis=0).astype(bf16)
    mid = jnp.concatenate([zero] + tiles + [zero], axis=0).astype(bf16)
    right = jnp.concatenate(tiles + [zero, zero], axis=0).astype(bf16)
    both = dot(jnp.concatenate([left, mid, right], axis=1), fir)
    filtered = both[:, :128] + both[:, 128:]
    size = jnp.abs(filtered)
    rows = count * ST
    parts = [halves(size[ST * i : ST * i + rows]) for i in range(3)]
    window = dot(jnp.concatenate([p[0] for p in parts] + [p[1] for p in parts], axis=1), box)
    normalized = filtered[ST : ST + rows] / (window * (1.0 / (2 * HW + 1)) + 1e-06)
    per = L // 128
    lanes = [
        jnp.concatenate(
            [normalized[(g * per + t) * ST : (g * per + t + 1) * ST] for g in range(SEGS)], axis=0
        )
        for t in range(per)
    ]
    spectra = dot(jnp.concatenate(lanes, axis=1).astype(bf16), dft)
    re, im = spectra[:, :NF], spectra[:, NF:]
    high, low = halves(jnp.sqrt(re * re + im * im))
    smooth = dot(high, near) + dot(low, near)
    factor = jnp.concatenate(masks, axis=0) / (smooth * (1.0 / (2 * WF + 1)) + 1e-06)
    return (re * factor).astype(bf16).astype(f32), (im * factor).astype(bf16).astype(f32)


def hour(ref):
    return [ref[:, 128 * i : 128 * (i + 1)].astype(f32) for i in range(SEGS * L // 128)]


def kernel(
    raw_hbm, mask_hbm, order_hbm, fir_hbm, box_hbm, dft_hbm, near_hbm, lag_hbm, out_ref,
    mask_ref, order_ref, fir_ref, box_ref, dft_ref, near_ref, lag_ref,
    own, own_mask, slots1, cand, slots2, picked, source,
    mslots1, mcand, mslots2, mpicked, source_mask, station, stack,
    copy_sem, pair_sem, mpair_sem, one_sem, two_sem, three_sem, mone_sem, mtwo_sem, mthree_sem,
):
    half = lax.axis_index("section")
    blk = lax.axis_index("blk")
    me = (blk // 16) * 2 + blk % 2
    z = (blk // 2) % DEPTH

    def device(section, plane, depth):
        return (section, (plane // 2) * 16 + depth * 2 + plane % 2)

    def remote(src, dst, sems, to):
        return pltpu.make_async_remote_copy(
            src_ref=src, dst_ref=dst, send_sem=sems.at[0], recv_sem=sems.at[1],
            device_id=to, device_id_type=MESH,
        )

    def wait(ref, sem):
        pltpu.make_async_copy(ref, ref, sem).wait()

    def lanes(start, size):
        return pl.ds(pl.multiple_of(start, 128), size)

    mine = own.at[:, lanes(half * HALF, HALF)]
    copies = [
        pltpu.make_async_copy(src, dst, copy_sem.at[i])
        for i, (src, dst) in enumerate(
            (
                (raw_hbm, mine), (mask_hbm, mask_ref), (order_hbm, order_ref),
                (fir_hbm, fir_ref), (box_hbm, box_ref), (dft_hbm, dft_ref),
                (near_hbm, near_ref), (lag_hbm, lag_ref),
            )
        )
    ]
    for copy in copies:
        copy.start()

    mates = [lax.rem(me + i, PLANE) for i in range(1, PLANE)]
    both = [(lax.rem(half + i, 2), lax.rem(me + j, PLANE)) for i in range(2) for j in range(PLANE)]
    both = both[1:]
    column = [lax.rem(z + i, DEPTH) for i in range(1, DEPTH)]

    barrier = pltpu.get_barrier_semaphore()
    for section, mate in both:
        pl.semaphore_signal(
            barrier, inc=1, device_id=device(section, mate, z), device_id_type=MESH
        )
    for depth in column:
        pl.semaphore_signal(barrier, inc=1, device_id=device(half, me, depth), device_id_type=MESH)

    copies[1].wait()
    flags = mask_ref[...].astype(f32)
    eye = lax.broadcasted_iota(jnp.int32, (ST, ST), 0) == lax.broadcasted_iota(
        jnp.int32, (ST, ST), 1
    )
    lane = lax.broadcasted_iota(jnp.int32, (ST, 128), 1)
    tile = jnp.zeros((ST, 128), f32)
    for g in range(SEG):
        row = jnp.where(eye, jnp.broadcast_to(flags[g : g + 1], (ST, ST)), 0.0)
        tile = jnp.where(lane == g, jnp.sum(row, axis=1, keepdims=True), tile)
    own_mask[half] = tile.astype(bf16)
    copies[0].wait()
    pl.semaphore_wait(barrier, len(both) + len(column))

    def piece(q):
        return own.at[:, lanes(half * HALF + q * PIECE, PIECE)]

    for mate in mates:
        remote(piece(mate), slots1.at[me], one_sem, device(half, mate, z)).start()

    @pl.when(me != 0)
    def _():
        remote(own_mask.at[half], mslots1.at[me], mone_sem, device(half, 0, z)).start()

    other = device(1 - half, me, z)
    pair = [
        remote(mine, mine, pair_sem, other),
        remote(own_mask.at[half], own_mask.at[half], mpair_sem, other),
    ]
    for copy in pair:
        copy.start()
    slots1[me] = own[:, lanes(half * HALF + me * PIECE, PIECE)]
    copies[2].wait()
    root = [order_ref[i] for i in range(2)]
    root_plane = [(r // 16) * 2 + r % 2 for r in root]
    root_z = [(r // 2) % DEPTH for r in root]

    wait(slots1.at[pl.ds(0, PLANE - 1)], one_sem.at[1])
    for i in range(2):
        cand[i] = slots1[root_plane[i]]
    for depth in column:
        remote(cand, slots2.at[z], two_sem, device(half, me, depth)).start()
    slots2[z] = cand[...]

    @pl.when(me == 0)
    def _():
        mslots1[0] = own_mask[half]
        wait(mslots1.at[pl.ds(0, PLANE - 1)], mone_sem.at[1])
        for i in range(2):
            mcand[i] = mslots1[root_plane[i]]
        for depth in column:
            remote(mcand, mslots2.at[z], mtwo_sem, device(half, me, depth)).start()
        mslots2[z] = mcand[...]

    for copy in pair:
        copy.wait()
    for i in range(3, 7):
        copies[i].wait()
    weights = (fir_ref, box_ref, dft_ref, near_ref)
    masks = [own_mask[i].astype(f32) for i in range(2)]
    columns = [m[:, g : g + 1] for m in masks for g in range(SEG)]
    station[0], station[1] = whiten(hour(own), columns, *[w[...] for w in weights])

    wait(slots2.at[pl.ds(0, DEPTH - 1)], two_sem.at[1])
    for i in range(2):
        picked[i] = slots2[root_z[i], i]
    place = lanes(half * HALF + me * PIECE, PIECE)
    for section, mate in both:
        remote(
            picked.at[section], source.at[:, place], three_sem, device(section, mate, z)
        ).start()
    source[:, place] = picked[half]

    @pl.when(me == 0)
    def _():
        wait(mslots2.at[pl.ds(0, DEPTH - 1)], mtwo_sem.at[1])
        for i in range(2):
            mpicked[i] = mslots2[root_z[i], i]
        for section, mate in both:
            remote(
                mpicked.at[section], source_mask.at[half], mthree_sem, device(section, mate, z)
            ).start()
        source_mask[half] = mpicked[half]

    copies[7].wait()
    wait(source.at[:, pl.ds(0, 31 * PIECE)], three_sem.at[1])

    @pl.when(me == 0)
    def _():
        wait(source_mask.at[0], mthree_sem.at[1])

    @pl.when(me != 0)
    def _():
        wait(source_mask, mthree_sem.at[1])

    theirs = [source_mask[i].astype(f32) for i in range(2)]
    columns = [m[:, g : g + 1] for m in theirs for g in range(SEG)]
    source_re, source_im = whiten(hour(source), columns, *[w[...] for w in weights])
    for k in range(KT):
        part = slice(128 * k, 128 * (k + 1))
        real = [jnp.zeros((ST, 128), f32)] * ST
        imag = [jnp.zeros((ST, 128), f32)] * ST
        for g in range(SEGS):
            re_s = station[0, ST * g : ST * (g + 1), part]
            im_s = station[1, ST * g : ST * (g + 1), part]
            for n in range(ST):
                re_n = source_re[ST * g + n : ST * g + n + 1, part]
                im_n = source_im[ST * g + n : ST * g + n + 1, part]
                real[n] = real[n] + (re_s * re_n + im_s * im_n)
                imag[n] = imag[n] + (im_s * re_n - re_s * im_n)
        for n in range(ST):
            stack[ST * n : ST * (n + 1), 128 * k : 128 * (k + 1)] = real[n]
            stack[ST * n : ST * (n + 1), NF + 128 * k : NF + 128 * (k + 1)] = imag[n]
    high, low = halves(stack[...])
    first = dot(high, lag_ref[...])
    lagged = first[:, :LAGS] + first[:, LAGS:] + dot(low, lag_ref[:, :LAGS])
    for n in range(ST):
        count = masks[0] * theirs[0][n : n + 1] + masks[1] * theirs[1][n : n + 1]
        count = jnp.maximum(jnp.sum(count, axis=1, keepdims=True), 1.0)
        out_ref[n] = lagged[ST * n : ST * (n + 1)] / count

    wait(slots1.at[pl.ds(0, PLANE - 1)], one_sem.at[0])
    wait(slots2.at[pl.ds(0, DEPTH - 1)], two_sem.at[0])
    wait(source.at[:, pl.ds(0, 31 * PIECE)], three_sem.at[0])

    @pl.when(me == 0)
    def _():
        wait(mslots2.at[pl.ds(0, DEPTH - 1)], mtwo_sem.at[0])
        wait(source.at[:, pl.ds(0, 31 * 128)], mthree_sem.at[0])

    @pl.when(me != 0)
    def _():
        wait(mslots1.at[0], mone_sem.at[0])


def shards(raw_traces, valid_mask, block_order):
    constants = [jnp.asarray(t) for t in tables()]
    hbm = pl.BlockSpec(memory_space=pl.ANY)
    wide = (ST, PIECE)
    flag = (ST, 128)
    pair = pltpu.SemaphoreType.DMA((2,))
    return pl.pallas_call(
        kernel,
        out_shape=jax.ShapeDtypeStruct((ST, ST, LAGS), f32),
        in_specs=[hbm] * (3 + len(constants)),
        out_specs=pl.BlockSpec(memory_space=pltpu.VMEM),
        scratch_shapes=[
            pltpu.VMEM((SEG, ST), jnp.int32),
            pltpu.SMEM(block_order.shape, jnp.int32),
        ]
        + [pltpu.VMEM(c.shape, c.dtype) for c in constants]
        + [
            pltpu.VMEM((ST, 2 * HALF), bf16),
            pltpu.VMEM((2,) + flag, bf16),
            pltpu.VMEM((PLANE,) + wide, bf16),
            pltpu.VMEM((2,) + wide, bf16),
            pltpu.VMEM((DEPTH, 2) + wide, bf16),
            pltpu.VMEM((2,) + wide, bf16),
            pltpu.VMEM((ST, 2 * HALF), bf16),
            pltpu.VMEM((PLANE,) + flag, bf16),
            pltpu.VMEM((2,) + flag, bf16),
            pltpu.VMEM((DEPTH, 2) + flag, bf16),
            pltpu.VMEM((2,) + flag, bf16),
            pltpu.VMEM((2,) + flag, bf16),
            pltpu.VMEM((2, SEGS * ST, NF), f32),
            pltpu.VMEM((ST * ST, 2 * NF), f32),
            pltpu.SemaphoreType.DMA((3 + len(constants),)),
            pair, pair, pair, pair, pair, pair, pair, pair,
        ],
        compiler_params=pltpu.CompilerParams(
            collective_id=0, has_side_effects=True, vmem_limit_bytes=VMEM_KIB << 10
        ),
    )(raw_traces, valid_mask.T, block_order, *constants)


def solution(mesh):
    return jax.shard_map(
        shards,
        mesh=mesh,
        in_specs=(P("blk", "section"), P("blk", "section"), P()),
        out_specs=P("section", "blk", None),
        check_vma=False,
    )
```

time: 40.8 us -> 30.3 us (0.74)
  local copies, waits for them, and re-layouts: 8.23 us -> 1.47 us
  Pallas kernels: 32.2 us -> 28.7 us
    unnamed x16 -> x1, local copies, waits for them, and re-layouts: 8.23 us -> 1.47 us
    pallas_call x1, Pallas kernels: 32.2 us -> 28.7 us  [shards(): pl.pallas_call(kernel, out_shape=jax.ShapeDtypeStruct((ST, ST, LAGS), f32...]
where the time goes in v2:
time: 30.3 us; the launch traced here: 30.2 us
  Pallas kernels  28.7 us (95%)
  local copies, waits for them, and re-layouts  1.47 us (5%)
    pallas_call x1, Pallas kernels, shards(): pl.pallas_call(kernel, out_shape=jax.ShapeDtypeStruct((ST, ST, LAGS), f32...  28.7 us
    unnamed x1, local copies, waits for them, and re-layouts  1.47 us

profile of v2, /device:TPU:1, one launch (start us, length us, event | category | flops | bytes accessed | tf_op | source)
XLA Modules:
  0.0 30.2 jit_solution(10883759986309834717)
XLA Ops:
  0.0 28.7 %shard_map.82 = f32[8,8,256]{2,1,0:T(8,128)} custom-call(bf16[8,4096]{1,0:T(8,128)(2,1)} %raw_hbm.1, s32[4,8]{1,0:T(4,128)} %bitcast.1, s32[128]{0:T(128)} %order_hbm.1, bf16[384,256]{1,0:T(8,128)(2,1)} %constant.10.clone.fir_hbm, bf16[768,128]{1,0:T(8,128)(2,1)} %constant.11.clone.box_hbm, bf16[1024,768]{1,0:T(8,128)(2,1)} %constant.12.clone.dft_hbm, ...), custom_call_target="tpu_custom_call" | custom-call | tf_op jit(solution)/shard_map/pallas_call | solution.py:299
  28.7 1.5 %copy.10 = f32[8,8,256]{2,1,0:T(8,128)} copy(f32[8,8,256]{2,1,0:T(8,128)} %shard_map.82) | data formatting | bytes 131072

commit v3 on v2

--- a/solution.py
+++ b/solution.py
@@ -22,9 +22,11 @@
 HALF = SEG * L
 ST = 8
 PIECE = 256
-VMEM_KIB = 61920
+VMEM_KIB = 32768
 PLANE = 16
+COLUMNS = 8
 DEPTH = 8
+N_BLK = 128
 MESH = pl.DeviceIdType.MESH
 f32 = jnp.float32
 bf16 = jnp.bfloat16
@@ -98,13 +100,13 @@
 
 
 def hour(ref):
-    return [ref[:, 128 * i : 128 * (i + 1)].astype(f32) for i in range(SEGS * L // 128)]
+    return [ref[h, :, 128 * i : 128 * (i + 1)].astype(f32) for h in range(2) for i in range(HALF // 128)]
 
 
 def kernel(
     raw_hbm, mask_hbm, order_hbm, fir_hbm, box_hbm, dft_hbm, near_hbm, lag_hbm, out_ref,
     mask_ref, order_ref, fir_ref, box_ref, dft_ref, near_ref, lag_ref,
-    own, own_mask, slots1, cand, slots2, picked, source,
+    own, own_mask, slots1, cand, slots2, picked, source, bulk,
     mslots1, mcand, mslots2, mpicked, source_mask, station, stack,
     copy_sem, pair_sem, mpair_sem, one_sem, two_sem, three_sem, mone_sem, mtwo_sem, mthree_sem,
 ):
@@ -112,9 +114,16 @@
     blk = lax.axis_index("blk")
     me = (blk // 16) * 2 + blk % 2
     z = (blk // 2) % DEPTH
+    collects = me < COLUMNS
+    late = me >= COLUMNS
+    slot = half * COLUMNS + me % COLUMNS
+    keeps_masks = half * N_BLK + blk == z * 2
 
     def device(section, plane, depth):
         return (section, (plane // 2) * 16 + depth * 2 + plane % 2)
+
+    def collector(q):
+        return device(q // COLUMNS, q % COLUMNS, z)
 
     def remote(src, dst, sems, to):
         return pltpu.make_async_remote_copy(
@@ -125,10 +134,32 @@
     def wait(ref, sem):
         pltpu.make_async_copy(ref, ref, sem).wait()
 
-    def lanes(start, size):
-        return pl.ds(pl.multiple_of(start, 128), size)
-
-    mine = own.at[:, lanes(half * HALF, HALF)]
+    def lanes(q):
+        return pl.ds(pl.multiple_of(q * PIECE, PIECE), PIECE)
+
+    mates = [lax.rem(slot + i, PLANE) for i in range(1, PLANE)]
+    column = [lax.rem(z + i, DEPTH) for i in range(1, DEPTH)]
+    rest = [(i, COLUMNS + j) for j in range(COLUMNS) for i in range(2)]
+    other = device(1 - half, me, z)
+    barrier = pltpu.get_barrier_semaphore()
+
+    def signal(to):
+        pl.semaphore_signal(barrier, inc=1, device_id=to, device_id_type=MESH)
+
+    @pl.when(collects)
+    def _():
+        for depth in column:
+            signal(device(half, me, depth))
+        for mate in mates:
+            signal(collector(mate))
+        for section, plane in rest:
+            signal(device(section, plane, z))
+
+    @pl.when(late)
+    def _():
+        signal(other)
+
+    mine = own.at[half]
     copies = [
         pltpu.make_async_copy(src, dst, copy_sem.at[i])
         for i, (src, dst) in enumerate(
@@ -141,20 +172,6 @@
     ]
     for copy in copies:
         copy.start()
-
-    mates = [lax.rem(me + i, PLANE) for i in range(1, PLANE)]
-    both = [(lax.rem(half + i, 2), lax.rem(me + j, PLANE)) for i in range(2) for j in range(PLANE)]
-    both = both[1:]
-    column = [lax.rem(z + i, DEPTH) for i in range(1, DEPTH)]
-
-    barrier = pltpu.get_barrier_semaphore()
-    for section, mate in both:
-        pl.semaphore_signal(
-            barrier, inc=1, device_id=device(section, mate, z), device_id_type=MESH
-        )
-    for depth in column:
-        pl.semaphore_signal(barrier, inc=1, device_id=device(half, me, depth), device_id_type=MESH)
-
     copies[1].wait()
     flags = mask_ref[...].astype(f32)
     eye = lax.broadcasted_iota(jnp.int32, (ST, ST), 0) == lax.broadcasted_iota(
@@ -167,44 +184,65 @@
         tile = jnp.where(lane == g, jnp.sum(row, axis=1, keepdims=True), tile)
     own_mask[half] = tile.astype(bf16)
     copies[0].wait()
-    pl.semaphore_wait(barrier, len(both) + len(column))
+
+    @pl.when(collects)
+    def _():
+        pl.semaphore_wait(barrier, len(column) + len(mates))
+
+    @pl.when(late)
+    def _():
+        pl.semaphore_wait(barrier, PLANE + 1)
 
     def piece(q):
-        return own.at[:, lanes(half * HALF + q * PIECE, PIECE)]
+        return remote(own.at[half, :, lanes(q)], slots1.at[half, me], one_sem, collector(q))
 
     for mate in mates:
-        remote(piece(mate), slots1.at[me], one_sem, device(half, mate, z)).start()
-
-    @pl.when(me != 0)
-    def _():
-        remote(own_mask.at[half], mslots1.at[me], mone_sem, device(half, 0, z)).start()
-
-    other = device(1 - half, me, z)
+        piece(mate).start()
+
+    @pl.when(late)
+    def _():
+        piece(slot).start()
+
     pair = [
         remote(mine, mine, pair_sem, other),
         remote(own_mask.at[half], own_mask.at[half], mpair_sem, other),
     ]
     for copy in pair:
         copy.start()
-    slots1[me] = own[:, lanes(half * HALF + me * PIECE, PIECE)]
+
+    @pl.when(jnp.logical_not(keeps_masks))
+    def _():
+        remote(own_mask.at[half], mslots1.at[half, me], mone_sem, collector(0)).start()
+
     copies[2].wait()
     root = [order_ref[i] for i in range(2)]
     root_plane = [(r // 16) * 2 + r % 2 for r in root]
     root_z = [(r // 2) % DEPTH for r in root]
-
-    wait(slots1.at[pl.ds(0, PLANE - 1)], one_sem.at[1])
-    for i in range(2):
-        cand[i] = slots1[root_plane[i]]
-    for depth in column:
-        remote(cand, slots2.at[z], two_sem, device(half, me, depth)).start()
-    slots2[z] = cand[...]
-
-    @pl.when(me == 0)
-    def _():
-        mslots1[0] = own_mask[half]
-        wait(mslots1.at[pl.ds(0, PLANE - 1)], mone_sem.at[1])
+    others = [(q // COLUMNS, collector(q)) for q in mates]
+    others = others + [(section, device(section, plane, z)) for section, plane in rest]
+
+    @pl.when(collects)
+    def _():
+        slots1[half, me] = own[half, :, lanes(slot)]
+        wait(source.at[:, :, pl.ds(0, 31 * PIECE // 2)], one_sem.at[1])
         for i in range(2):
-            mcand[i] = mslots1[root_plane[i]]
+            for h in range(2):
+                cand[i, h] = slots1[h, root_plane[i]]
+        for depth in range(DEPTH):
+
+            @pl.when(z != depth)
+            def _(depth=depth):
+                remote(cand, slots2.at[z], two_sem, device(half, me, depth)).start()
+
+        slots2[z] = cand[...]
+
+    @pl.when(keeps_masks)
+    def _():
+        mslots1[0, 0] = own_mask[0]
+        wait(source.at[0, :, pl.ds(0, 31 * 128)], mone_sem.at[1])
+        for i in range(2):
+            for h in range(2):
+                mcand[i, h] = mslots1[h, root_plane[i]]
         for depth in column:
             remote(mcand, mslots2.at[z], mtwo_sem, device(half, me, depth)).start()
         mslots2[z] = mcand[...]
@@ -218,35 +256,35 @@
     columns = [m[:, g : g + 1] for m in masks for g in range(SEG)]
     station[0], station[1] = whiten(hour(own), columns, *[w[...] for w in weights])
 
-    wait(slots2.at[pl.ds(0, DEPTH - 1)], two_sem.at[1])
-    for i in range(2):
-        picked[i] = slots2[root_z[i], i]
-    place = lanes(half * HALF + me * PIECE, PIECE)
-    for section, mate in both:
-        remote(
-            picked.at[section], source.at[:, place], three_sem, device(section, mate, z)
-        ).start()
-    source[:, place] = picked[half]
-
-    @pl.when(me == 0)
+    @pl.when(collects)
+    def _():
+        wait(slots2.at[pl.ds(0, DEPTH - 1)], two_sem.at[1])
+        for i in range(2):
+            picked[i] = slots2[root_z[i], i]
+        for section, to in others:
+            remote(picked.at[section], source.at[:, :, lanes(slot)], three_sem, to).start()
+        source[:, :, lanes(slot)] = picked[half]
+
+    @pl.when(keeps_masks)
     def _():
         wait(mslots2.at[pl.ds(0, DEPTH - 1)], mtwo_sem.at[1])
         for i in range(2):
             mpicked[i] = mslots2[root_z[i], i]
-        for section, mate in both:
-            remote(
-                mpicked.at[section], source_mask.at[half], mthree_sem, device(section, mate, z)
-            ).start()
-        source_mask[half] = mpicked[half]
+        for section, to in others:
+            remote(mpicked.at[section], source_mask, mthree_sem, to).start()
+        source_mask[...] = mpicked[0]
 
     copies[7].wait()
-    wait(source.at[:, pl.ds(0, 31 * PIECE)], three_sem.at[1])
-
-    @pl.when(me == 0)
-    def _():
-        wait(source_mask.at[0], mthree_sem.at[1])
-
-    @pl.when(me != 0)
+
+    @pl.when(collects)
+    def _():
+        wait(source.at[:, :, pl.ds(0, 15 * PIECE)], three_sem.at[1])
+
+    @pl.when(late)
+    def _():
+        wait(source, three_sem.at[1])
+
+    @pl.when(jnp.logical_not(keeps_masks))
     def _():
         wait(source_mask, mthree_sem.at[1])
 
@@ -276,18 +314,24 @@
         count = jnp.maximum(jnp.sum(count, axis=1, keepdims=True), 1.0)
         out_ref[n] = lagged[ST * n : ST * (n + 1)] / count
 
-    wait(slots1.at[pl.ds(0, PLANE - 1)], one_sem.at[0])
-    wait(slots2.at[pl.ds(0, DEPTH - 1)], two_sem.at[0])
-    wait(source.at[:, pl.ds(0, 31 * PIECE)], three_sem.at[0])
-
-    @pl.when(me == 0)
+    @pl.when(collects)
+    def _():
+        wait(source.at[0, :, pl.ds(0, 15 * PIECE)], one_sem.at[0])
+        wait(slots2.at[pl.ds(0, DEPTH - 1)], two_sem.at[0])
+        wait(bulk.at[pl.ds(0, 31)], three_sem.at[0])
+
+    @pl.when(late)
+    def _():
+        wait(source.at[0], one_sem.at[0])
+
+    @pl.when(keeps_masks)
     def _():
         wait(mslots2.at[pl.ds(0, DEPTH - 1)], mtwo_sem.at[0])
-        wait(source.at[:, pl.ds(0, 31 * 128)], mthree_sem.at[0])
-
-    @pl.when(me != 0)
-    def _():
-        wait(mslots1.at[0], mone_sem.at[0])
+        wait(source.at[:, :, pl.ds(0, 31 * 128)], mthree_sem.at[0])
+
+    @pl.when(jnp.logical_not(keeps_masks))
+    def _():
+        wait(own_mask.at[0], mone_sem.at[0])
 
 
 def shards(raw_traces, valid_mask, block_order):
@@ -307,17 +351,18 @@
         ]
         + [pltpu.VMEM(c.shape, c.dtype) for c in constants]
         + [
-            pltpu.VMEM((ST, 2 * HALF), bf16),
+            pltpu.VMEM((2, ST, HALF), bf16),
             pltpu.VMEM((2,) + flag, bf16),
-            pltpu.VMEM((PLANE,) + wide, bf16),
-            pltpu.VMEM((2,) + wide, bf16),
-            pltpu.VMEM((DEPTH, 2) + wide, bf16),
-            pltpu.VMEM((2,) + wide, bf16),
-            pltpu.VMEM((ST, 2 * HALF), bf16),
-            pltpu.VMEM((PLANE,) + flag, bf16),
-            pltpu.VMEM((2,) + flag, bf16),
-            pltpu.VMEM((DEPTH, 2) + flag, bf16),
-            pltpu.VMEM((2,) + flag, bf16),
+            pltpu.VMEM((2, PLANE) + wide, bf16),
+            pltpu.VMEM((2, 2) + wide, bf16),
+            pltpu.VMEM((DEPTH, 2, 2) + wide, bf16),
+            pltpu.VMEM((2, 2) + wide, bf16),
+            pltpu.VMEM((2, ST, HALF), bf16),
+            pltpu.VMEM((2 * PLANE, 2) + wide, bf16),
+            pltpu.VMEM((2, PLANE) + flag, bf16),
+            pltpu.VMEM((2, 2) + flag, bf16),
+            pltpu.VMEM((DEPTH, 2, 2) + flag, bf16),
+            pltpu.VMEM((2, 2) + flag, bf16),
             pltpu.VMEM((2,) + flag, bf16),
             pltpu.VMEM((2, SEGS * ST, NF), f32),
             pltpu.VMEM((ST * ST, 2 * NF), f32),
@@ -327,7 +372,12 @@
         compiler_params=pltpu.CompilerParams(
             collective_id=0, has_side_effects=True, vmem_limit_bytes=VMEM_KIB << 10
         ),
-    )(raw_traces, valid_mask.T, block_order, *constants)
+    )(
+        *[
+            pltpu.with_memory_space_constraint(a, pltpu.HBM)
+            for a in (raw_traces, valid_mask.T, block_order, *constants)
+        ]
+    )
 
 
 def solution(mesh):

time: 30.3 us -> 27.3 us (0.901)
  Pallas kernels: 28.7 us -> 26.6 us
  local copies, waits for them, and re-layouts: 1.47 us -> 0.63 us
    pallas_call x1, Pallas kernels: 28.7 us -> 26.6 us  [shards(): pl.pallas_call(kernel, out_shape=jax.ShapeDtypeStruct((ST, ST, LAGS), f32...]
    unnamed x1, local copies, waits for them, and re-layouts: 1.47 us -> 0.63 us
where the time goes in v3:
time: 27.3 us; the launch traced here: 27.2 us
  Pallas kernels  26.6 us (97%)
  local copies, waits for them, and re-layouts  0.63 us (2%)
    pallas_call x1, Pallas kernels, shards(): pl.pallas_call(kernel, out_shape=jax.ShapeDtypeStruct((ST, ST, LAGS), f32...  26.6 us
    unnamed x1, local copies, waits for them, and re-layouts  0.63 us

profile of v3, /device:TPU:1, one launch (start us, length us, event | category | flops | bytes accessed | tf_op | source)
XLA Modules:
  0.0 27.2 jit_solution(16584229825655377850)
XLA Ops:
  0.0 26.6 %shard_map.82 = f32[8,8,256]{2,1,0:T(8,128)S(1)} custom-call(bf16[8,4096]{1,0:T(8,128)(2,1)} %raw_hbm.1, s32[4,8]{1,0:T(4,128)} %bitcast.1, s32[128]{0:T(128)} %order_hbm.1, bf16[384,256]{1,0:T(8,128)(2,1)} %constant.10.clone.fir_hbm, bf16[768,128]{1,0:T(8,128)(2,1)} %constant.11.clone.box_hbm, bf16[1024,768]{1,0:T(8,128)(2,1)} %constant.12.clone.dft_hbm, ...), custom_call_target="tpu_custom_call" | custom-call | tf_op jit(solution)/shard_map/pallas_call | solution.py:343
  26.6 0.6 %copy.10 = f32[8,8,256]{2,1,0:T(8,128)} copy(f32[8,8,256]{2,1,0:T(8,128)S(1)} %shard_map.82) | data formatting | bytes 131072

commit v4 on v3

--- a/solution.py
+++ b/solution.py
@@ -24,10 +24,11 @@
 PIECE = 256
 VMEM_KIB = 32768
 PLANE = 16
-COLUMNS = 8
 DEPTH = 8
 N_BLK = 128
 MESH = pl.DeviceIdType.MESH
+CHIPS = [(x, 0) for x in range(4)] + [(0, y) for y in range(1, 4)] + [(1, 1)]
+REST = [(x, y) for y in range(4) for x in range(4) if (x, y) not in CHIPS]
 f32 = jnp.float32
 bf16 = jnp.bfloat16
 
@@ -113,17 +114,21 @@
     half = lax.axis_index("section")
     blk = lax.axis_index("blk")
     me = (blk // 16) * 2 + blk % 2
+    x = (blk // 64) * 2 + half
+    y = (blk // 16) % 4
     z = (blk // 2) % DEPTH
-    collects = me < COLUMNS
-    late = me >= COLUMNS
-    slot = half * COLUMNS + me % COLUMNS
+    core = blk % 2
+    collects = x * y < 2
+    late = x * y >= 2
+    chip = x + y + 3 * ((y + 3) // 4) + 2 * x * y
+    slot = jnp.where(collects, chip * 2 + core, PLANE)
     keeps_masks = half * N_BLK + blk == z * 2
 
-    def device(section, plane, depth):
-        return (section, (plane // 2) * 16 + depth * 2 + plane % 2)
-
-    def collector(q):
-        return device(q // COLUMNS, q % COLUMNS, z)
+    def device(chip, core):
+        return (chip[0] % 2, (chip[0] // 2) * 64 + chip[1] * 16 + core + z * 2)
+
+    collectors = [device(chip, i) for chip in CHIPS for i in range(2)]
+    rest = [device(chip, i) for chip in REST for i in range(2)]
 
     def remote(src, dst, sems, to):
         return pltpu.make_async_remote_copy(
@@ -135,12 +140,12 @@
         pltpu.make_async_copy(ref, ref, sem).wait()
 
     def lanes(q):
-        return pl.ds(pl.multiple_of(q * PIECE, PIECE), PIECE)
-
-    mates = [lax.rem(slot + i, PLANE) for i in range(1, PLANE)]
-    column = [lax.rem(z + i, DEPTH) for i in range(1, DEPTH)]
-    rest = [(i, COLUMNS + j) for j in range(COLUMNS) for i in range(2)]
-    other = device(1 - half, me, z)
+        return pl.ds(q * PIECE if isinstance(q, int) else pl.multiple_of(q * PIECE, PIECE), PIECE)
+
+    def above(depth):
+        return (half, blk + (depth - z) * 2)
+
+    other = (1 - half, blk)
     barrier = pltpu.get_barrier_semaphore()
 
     def signal(to):
@@ -148,12 +153,20 @@
 
     @pl.when(collects)
     def _():
-        for depth in column:
-            signal(device(half, me, depth))
-        for mate in mates:
-            signal(collector(mate))
-        for section, plane in rest:
-            signal(device(section, plane, z))
+        for depth in range(DEPTH):
+
+            @pl.when(z != depth)
+            def _(depth=depth):
+                signal(above(depth))
+
+        for q, to in enumerate(collectors):
+
+            @pl.when(slot != q)
+            def _(to=to):
+                signal(to)
+
+        for to in rest:
+            signal(to)
 
     @pl.when(late)
     def _():
@@ -185,23 +198,27 @@
     own_mask[half] = tile.astype(bf16)
     copies[0].wait()
 
-    @pl.when(collects)
-    def _():
-        pl.semaphore_wait(barrier, len(column) + len(mates))
-
-    @pl.when(late)
+    @pl.when(collects & (y < 2))
+    def _():
+        pl.semaphore_wait(barrier, DEPTH - 1 + PLANE - 1)
+
+    @pl.when(collects & (y >= 2))
+    def _():
+        pl.semaphore_wait(barrier, DEPTH - 1 + PLANE)
+
+    @pl.when(late & (x < 2))
+    def _():
+        pl.semaphore_wait(barrier, PLANE)
+
+    @pl.when(late & (x >= 2))
     def _():
         pl.semaphore_wait(barrier, PLANE + 1)
 
-    def piece(q):
-        return remote(own.at[half, :, lanes(q)], slots1.at[half, me], one_sem, collector(q))
-
-    for mate in mates:
-        piece(mate).start()
-
-    @pl.when(late)
-    def _():
-        piece(slot).start()
+    for q, to in enumerate(collectors):
+
+        @pl.when(slot != q)
+        def _(q=q, to=to):
+            remote(own.at[half, :, lanes(q)], slots1.at[half, me], one_sem, to).start()
 
     pair = [
         remote(mine, mine, pair_sem, other),
@@ -212,14 +229,12 @@
 
     @pl.when(jnp.logical_not(keeps_masks))
     def _():
-        remote(own_mask.at[half], mslots1.at[half, me], mone_sem, collector(0)).start()
+        remote(own_mask.at[half], mslots1.at[half, me], mone_sem, collectors[0]).start()
 
     copies[2].wait()
     root = [order_ref[i] for i in range(2)]
     root_plane = [(r // 16) * 2 + r % 2 for r in root]
     root_z = [(r // 2) % DEPTH for r in root]
-    others = [(q // COLUMNS, collector(q)) for q in mates]
-    others = others + [(section, device(section, plane, z)) for section, plane in rest]
 
     @pl.when(collects)
     def _():
@@ -232,7 +247,7 @@
 
             @pl.when(z != depth)
             def _(depth=depth):
-                remote(cand, slots2.at[z], two_sem, device(half, me, depth)).start()
+                remote(cand, slots2.at[z], two_sem, above(depth)).start()
 
         slots2[z] = cand[...]
 
@@ -243,8 +258,12 @@
         for i in range(2):
             for h in range(2):
                 mcand[i, h] = mslots1[h, root_plane[i]]
-        for depth in column:
-            remote(mcand, mslots2.at[z], mtwo_sem, device(half, me, depth)).start()
+        for depth in range(DEPTH):
+
+            @pl.when(z != depth)
+            def _(depth=depth):
+                remote(mcand, mslots2.at[z], mtwo_sem, above(depth)).start()
+
         mslots2[z] = mcand[...]
 
     for copy in pair:
@@ -261,8 +280,14 @@
         wait(slots2.at[pl.ds(0, DEPTH - 1)], two_sem.at[1])
         for i in range(2):
             picked[i] = slots2[root_z[i], i]
-        for section, to in others:
-            remote(picked.at[section], source.at[:, :, lanes(slot)], three_sem, to).start()
+        for q, to in enumerate(collectors):
+
+            @pl.when(slot != q)
+            def _(to=to):
+                remote(picked.at[to[0]], source.at[:, :, lanes(slot)], three_sem, to).start()
+
+        for to in rest:
+            remote(picked.at[to[0]], source.at[:, :, lanes(slot)], three_sem, to).start()
         source[:, :, lanes(slot)] = picked[half]
 
     @pl.when(keeps_masks)
@@ -270,8 +295,8 @@
         wait(mslots2.at[pl.ds(0, DEPTH - 1)], mtwo_sem.at[1])
         for i in range(2):
             mpicked[i] = mslots2[root_z[i], i]
-        for section, to in others:
-            remote(mpicked.at[section], source_mask, mthree_sem, to).start()
+        for to in collectors[1:] + rest:
+            remote(mpicked.at[to[0]], source_mask, mthree_sem, to).start()
         source_mask[...] = mpicked[0]
 
     copies[7].wait()

time: 27.3 us -> 26.5 us (0.971)
  Pallas kernels: 26.6 us -> 25.8 us
    pallas_call x1, Pallas kernels: 26.6 us -> 25.8 us  [shards(): pl.pallas_call(kernel, out_shape=jax.ShapeDtypeStruct((ST, ST, LAGS), f32...]
where the time goes in v4:
time: 26.5 us; the launch traced here: 26.4 us
  Pallas kernels  25.8 us (97%)
  local copies, waits for them, and re-layouts  0.63 us (2%)
    pallas_call x1, Pallas kernels, shards(): pl.pallas_call(kernel, out_shape=jax.ShapeDtypeStruct((ST, ST, LAGS), f32...  25.8 us
    unnamed x1, local copies, waits for them, and re-layouts  0.63 us

profile of v4, /device:TPU:1, one launch (start us, length us, event | category | flops | bytes accessed | tf_op | source)
XLA Modules:
  0.0 26.4 jit_solution(8146410750814979291)
XLA Ops:
  0.0 25.8 %shard_map.82 = f32[8,8,256]{2,1,0:T(8,128)S(1)} custom-call(bf16[8,4096]{1,0:T(8,128)(2,1)} %raw_hbm.1, s32[4,8]{1,0:T(4,128)} %bitcast.1, s32[128]{0:T(128)} %order_hbm.1, bf16[384,256]{1,0:T(8,128)(2,1)} %constant.10.clone.fir_hbm, bf16[768,128]{1,0:T(8,128)(2,1)} %constant.11.clone.box_hbm, bf16[1024,768]{1,0:T(8,128)(2,1)} %constant.12.clone.dft_hbm, ...), custom_call_target="tpu_custom_call" | custom-call | tf_op jit(solution)/shard_map/pallas_call | solution.py:368
  25.8 0.6 %copy.10 = f32[8,8,256]{2,1,0:T(8,128)} copy(f32[8,8,256]{2,1,0:T(8,128)S(1)} %shard_map.82) | data formatting | bytes 131072

commit v5 on v4

--- a/solution.py
+++ b/solution.py
@@ -50,7 +50,6 @@
     band = np.where(np.abs(shift) <= half, taps[np.clip(shift + half, 0, TAPS - 1)], 0.0)
     fir = np.concatenate(split(band), axis=1)
     box = (np.abs(shift) <= HW).astype(ml_dtypes.bfloat16)
-    box = np.concatenate([box, box], axis=0)
     bins = BIN_LO + np.arange(NF)
     phase = (np.arange(L)[:, None] * bins[None, :]) % L * (2 * np.pi / L)
     dft = np.concatenate([np.cos(phase), -np.sin(phase)], axis=1)
@@ -73,17 +72,18 @@
 
 
 def whiten(tiles, masks, fir, box, dft, near):
-    count = len(tiles)
     zero = jnp.zeros((ST, 128), f32)
-    left = jnp.concatenate([zero, zero] + tiles, axis=0).astype(bf16)
-    mid = jnp.concatenate([zero] + tiles + [zero], axis=0).astype(bf16)
-    right = jnp.concatenate(tiles + [zero, zero], axis=0).astype(bf16)
-    both = dot(jnp.concatenate([left, mid, right], axis=1), fir)
+    rows = len(tiles) * ST
+    edge = rows + 2 * ST
+    padded = [zero, zero] + tiles + [zero, zero]
+    wide = jnp.concatenate(padded, axis=0).astype(bf16)
+    mid = jnp.concatenate(padded[1:-1], axis=0).astype(bf16)
+    both = dot(jnp.concatenate([wide[:edge], mid, wide[2 * ST :]], axis=1), fir)
     filtered = both[:, :128] + both[:, 128:]
     size = jnp.abs(filtered)
-    rows = count * ST
-    parts = [halves(size[ST * i : ST * i + rows]) for i in range(3)]
-    window = dot(jnp.concatenate([p[0] for p in parts] + [p[1] for p in parts], axis=1), box)
+    wide = size.astype(bf16)
+    mid = size[ST : ST + rows].astype(bf16)
+    window = dot(jnp.concatenate([wide[:rows], mid, wide[2 * ST :]], axis=1), box)
     normalized = filtered[ST : ST + rows] / (window * (1.0 / (2 * HW + 1)) + 1e-06)
     per = L // 128
     lanes = [
@@ -94,8 +94,7 @@
     ]
     spectra = dot(jnp.concatenate(lanes, axis=1).astype(bf16), dft)
     re, im = spectra[:, :NF], spectra[:, NF:]
-    high, low = halves(jnp.sqrt(re * re + im * im))
-    smooth = dot(high, near) + dot(low, near)
+    smooth = dot(jnp.sqrt(re * re + im * im).astype(bf16), near)
     factor = jnp.concatenate(masks, axis=0) / (smooth * (1.0 / (2 * WF + 1)) + 1e-06)
     return (re * factor).astype(bf16).astype(f32), (im * factor).astype(bf16).astype(f32)
 
@@ -153,20 +152,20 @@
 
     @pl.when(collects)
     def _():
+        for to in rest:
+            signal(to)
+
+        for q, to in enumerate(collectors):
+
+            @pl.when(slot != q)
+            def _(to=to):
+                signal(to)
+
         for depth in range(DEPTH):
 
             @pl.when(z != depth)
             def _(depth=depth):
                 signal(above(depth))
-
-        for q, to in enumerate(collectors):
-
-            @pl.when(slot != q)
-            def _(to=to):
-                signal(to)
-
-        for to in rest:
-            signal(to)
 
     @pl.when(late)
     def _():

time: 26.5 us -> 26 us (0.981)
  Pallas kernels: 25.8 us -> 25.2 us
    pallas_call x1, Pallas kernels: 25.8 us -> 25.2 us  [shards(): pl.pallas_call(kernel, out_shape=jax.ShapeDtypeStruct((ST, ST, LAGS), f32...]
where the time goes in v5:
time: 26 us; the launch traced here: 25.9 us
  Pallas kernels  25.2 us (97%)
  local copies, waits for them, and re-layouts  0.63 us (2%)
    pallas_call x1, Pallas kernels, shards(): pl.pallas_call(kernel, out_shape=jax.ShapeDtypeStruct((ST, ST, LAGS), f32...  25.2 us
    unnamed x1, local copies, waits for them, and re-layouts  0.63 us

profile of v5, /device:TPU:1, one launch (start us, length us, event | category | flops | bytes accessed | tf_op | source)
XLA Modules:
  0.0 25.9 jit_solution(12629783760874915569)
XLA Ops:
  0.0 25.2 %shard_map.82 = f32[8,8,256]{2,1,0:T(8,128)S(1)} custom-call(bf16[8,4096]{1,0:T(8,128)(2,1)} %raw_hbm.1, s32[4,8]{1,0:T(4,128)} %bitcast.1, s32[128]{0:T(128)} %order_hbm.1, bf16[384,256]{1,0:T(8,128)(2,1)} %constant.10.clone.fir_hbm, bf16[384,128]{1,0:T(8,128)(2,1)} %constant.11.clone.box_hbm, bf16[1024,768]{1,0:T(8,128)(2,1)} %constant.12.clone.dft_hbm, ...), custom_call_target="tpu_custom_call" | custom-call | tf_op jit(solution)/shard_map/pallas_call | solution.py:367
  25.2 0.6 %copy.10 = f32[8,8,256]{2,1,0:T(8,128)} copy(f32[8,8,256]{2,1,0:T(8,128)S(1)} %shard_map.82) | data formatting | bytes 131072

commit v6 on v5

--- a/solution.py
+++ b/solution.py
@@ -94,7 +94,9 @@
     ]
     spectra = dot(jnp.concatenate(lanes, axis=1).astype(bf16), dft)
     re, im = spectra[:, :NF], spectra[:, NF:]
-    smooth = dot(jnp.sqrt(re * re + im * im).astype(bf16), near)
+    high, low = halves(jnp.sqrt(re * re + im * im))
+    parts = dot(jnp.concatenate([high, low], axis=0), near)
+    smooth = parts[: SEGS * ST] + parts[SEGS * ST :]
     factor = jnp.concatenate(masks, axis=0) / (smooth * (1.0 / (2 * WF + 1)) + 1e-06)
     return (re * factor).astype(bf16).astype(f32), (im * factor).astype(bf16).astype(f32)
 

time: 26 us -> 26 us (level)
  no operation moved by 1% of the time
where the time goes in v6:
time: 26 us; the launch traced here: 25.9 us
  Pallas kernels  25.3 us (97%)
  local copies, waits for them, and re-layouts  0.63 us (2%)
    pallas_call x1, Pallas kernels, shards(): pl.pallas_call(kernel, out_shape=jax.ShapeDtypeStruct((ST, ST, LAGS), f32...  25.3 us
    unnamed x1, local copies, waits for them, and re-layouts  0.63 us

profile of v6, /device:TPU:1, one launch (start us, length us, event | category | flops | bytes accessed | tf_op | source)
XLA Modules:
  0.0 25.9 jit_solution(12215590636301572990)
XLA Ops:
  0.0 25.3 %shard_map.82 = f32[8,8,256]{2,1,0:T(8,128)S(1)} custom-call(bf16[8,4096]{1,0:T(8,128)(2,1)} %raw_hbm.1, s32[4,8]{1,0:T(4,128)} %bitcast.1, s32[128]{0:T(128)} %order_hbm.1, bf16[384,256]{1,0:T(8,128)(2,1)} %constant.10.clone.fir_hbm, bf16[384,128]{1,0:T(8,128)(2,1)} %constant.11.clone.box_hbm, bf16[1024,768]{1,0:T(8,128)(2,1)} %constant.12.clone.dft_hbm, ...), custom_call_target="tpu_custom_call" | custom-call | tf_op jit(solution)/shard_map/pallas_call | solution.py:369
  25.3 0.6 %copy.10 = f32[8,8,256]{2,1,0:T(8,128)} copy(f32[8,8,256]{2,1,0:T(8,128)S(1)} %shard_map.82) | data formatting | bytes 131072

commit v7 on v6

--- a/solution.py
+++ b/solution.py
@@ -28,7 +28,7 @@
 N_BLK = 128
 MESH = pl.DeviceIdType.MESH
 CHIPS = [(x, 0) for x in range(4)] + [(0, y) for y in range(1, 4)] + [(1, 1)]
-REST = [(x, y) for y in range(4) for x in range(4) if (x, y) not in CHIPS]
+REST = [(1, 2), (2, 1), (3, 1), (2, 2), (3, 2), (1, 3), (2, 3), (3, 3)]
 f32 = jnp.float32
 bf16 = jnp.bfloat16
 
@@ -49,7 +49,8 @@
     shift = np.arange(128)[None, :] + 128 - np.arange(384)[:, None]
     band = np.where(np.abs(shift) <= half, taps[np.clip(shift + half, 0, TAPS - 1)], 0.0)
     fir = np.concatenate(split(band), axis=1)
-    box = (np.abs(shift) <= HW).astype(ml_dtypes.bfloat16)
+    apart = np.arange(256)[None, :] + 128 - np.arange(512)[:, None]
+    box = (np.abs(apart) <= HW).astype(ml_dtypes.bfloat16)
     bins = BIN_LO + np.arange(NF)
     phase = (np.arange(L)[:, None] * bins[None, :]) % L * (2 * np.pi / L)
     dft = np.concatenate([np.cos(phase), -np.sin(phase)], axis=1)
@@ -73,22 +74,29 @@
 
 def whiten(tiles, masks, fir, box, dft, near):
     zero = jnp.zeros((ST, 128), f32)
-    rows = len(tiles) * ST
-    edge = rows + 2 * ST
+    edge = (len(tiles) + 2) * ST
     padded = [zero, zero] + tiles + [zero, zero]
     wide = jnp.concatenate(padded, axis=0).astype(bf16)
     mid = jnp.concatenate(padded[1:-1], axis=0).astype(bf16)
     both = dot(jnp.concatenate([wide[:edge], mid, wide[2 * ST :]], axis=1), fir)
     filtered = both[:, :128] + both[:, 128:]
     size = jnp.abs(filtered)
-    wide = size.astype(bf16)
-    mid = size[ST : ST + rows].astype(bf16)
-    window = dot(jnp.concatenate([wide[:rows], mid, wide[2 * ST :]], axis=1), box)
-    normalized = filtered[ST : ST + rows] / (window * (1.0 / (2 * HW + 1)) + 1e-06)
+    count = len(tiles)
+    around = [
+        jnp.concatenate([size[ST * (i + j) : ST * (i + j + 1)] for j in range(0, count, 2)], axis=0)
+        for i in range(4)
+    ]
+    window = dot(jnp.concatenate([a.astype(bf16) for a in around], axis=1), box)
+    window = window * (1.0 / (2 * HW + 1)) + 1e-06
+    normalized = [
+        filtered[ST * (i + 1) : ST * (i + 2)]
+        / window[ST * (i // 2) : ST * (i // 2 + 1), 128 * (i % 2) : 128 * (i % 2 + 1)]
+        for i in range(count)
+    ]
     per = L // 128
     lanes = [
         jnp.concatenate(
-            [normalized[(g * per + t) * ST : (g * per + t + 1) * ST] for g in range(SEGS)], axis=0
+            [normalized[g * per + t] for g in range(SEGS)], axis=0
         )
         for t in range(per)
     ]

time: 26 us -> 26 us (level)
  no operation moved by 1% of the time
where the time goes in v7:
time: 26 us; the launch traced here: 25.9 us
  Pallas kernels  25.2 us (97%)
  local copies, waits for them, and re-layouts  0.63 us (2%)
    pallas_call x1, Pallas kernels, shards(): pl.pallas_call(kernel, out_shape=jax.ShapeDtypeStruct((ST, ST, LAGS), f32...  25.2 us
    unnamed x1, local copies, waits for them, and re-layouts  0.63 us

profile of v7, /device:TPU:1, one launch (start us, length us, event | category | flops | bytes accessed | tf_op | source)
XLA Modules:
  0.0 25.9 jit_solution(12567468874275869163)
XLA Ops:
  0.0 25.2 %shard_map.82 = f32[8,8,256]{2,1,0:T(8,128)S(1)} custom-call(bf16[8,4096]{1,0:T(8,128)(2,1)} %raw_hbm.1, s32[4,8]{1,0:T(4,128)} %bitcast.1, s32[128]{0:T(128)} %order_hbm.1, bf16[384,256]{1,0:T(8,128)(2,1)} %constant.10.clone.fir_hbm, bf16[512,256]{1,0:T(8,128)(2,1)} %constant.11.clone.box_hbm, bf16[1024,768]{1,0:T(8,128)(2,1)} %constant.12.clone.dft_hbm, ...), custom_call_target="tpu_custom_call" | custom-call | tf_op jit(solution)/shard_map/pallas_call | solution.py:377
  25.3 0.6 %copy.10 = f32[8,8,256]{2,1,0:T(8,128)} copy(f32[8,8,256]{2,1,0:T(8,128)S(1)} %shard_map.82) | data formatting | bytes 131072

commit v8 on v7

--- a/solution.py
+++ b/solution.py
@@ -341,8 +341,9 @@
             stack[ST * n : ST * (n + 1), 128 * k : 128 * (k + 1)] = real[n]
             stack[ST * n : ST * (n + 1), NF + 128 * k : NF + 128 * (k + 1)] = imag[n]
     high, low = halves(stack[...])
-    first = dot(high, lag_ref[...])
-    lagged = first[:, :LAGS] + first[:, LAGS:] + dot(low, lag_ref[:, :LAGS])
+    parts = dot(jnp.concatenate([high, low], axis=0), lag_ref[...])
+    upper = parts[: ST * ST]
+    lagged = upper[:, :LAGS] + upper[:, LAGS:] + parts[ST * ST :, :LAGS]
     for n in range(ST):
         count = masks[0] * theirs[0][n : n + 1] + masks[1] * theirs[1][n : n + 1]
         count = jnp.maximum(jnp.sum(count, axis=1, keepdims=True), 1.0)

time: 26 us -> 25.9 us (level)
  no operation moved by 1% of the time
where the time goes in v8:
time: 25.9 us; the launch traced here: 25.8 us
  Pallas kernels  25.2 us (97%)
  local copies, waits for them, and re-layouts  0.63 us (2%)
    pallas_call x1, Pallas kernels, shards(): pl.pallas_call(kernel, out_shape=jax.ShapeDtypeStruct((ST, ST, LAGS), f32...  25.2 us
    unnamed x1, local copies, waits for them, and re-layouts  0.63 us

profile of v8, /device:TPU:1, one launch (start us, length us, event | category | flops | bytes accessed | tf_op | source)
XLA Modules:
  0.0 25.8 jit_solution(16549558518092347914)
XLA Ops:
  0.0 25.2 %shard_map.82 = f32[8,8,256]{2,1,0:T(8,128)S(1)} custom-call(bf16[8,4096]{1,0:T(8,128)(2,1)} %raw_hbm.1, s32[4,8]{1,0:T(4,128)} %bitcast.1, s32[128]{0:T(128)} %order_hbm.1, bf16[384,256]{1,0:T(8,128)(2,1)} %constant.10.clone.fir_hbm, bf16[512,256]{1,0:T(8,128)(2,1)} %constant.11.clone.box_hbm, bf16[1024,768]{1,0:T(8,128)(2,1)} %constant.12.clone.dft_hbm, ...), custom_call_target="tpu_custom_call" | custom-call | tf_op jit(solution)/shard_map/pallas_call | solution.py:378
  25.2 0.6 %copy.10 = f32[8,8,256]{2,1,0:T(8,128)} copy(f32[8,8,256]{2,1,0:T(8,128)S(1)} %shard_map.82) | data formatting | bytes 131072

commit v9 on v8

--- a/solution.py
+++ b/solution.py
@@ -105,8 +105,13 @@
     high, low = halves(jnp.sqrt(re * re + im * im))
     parts = dot(jnp.concatenate([high, low], axis=0), near)
     smooth = parts[: SEGS * ST] + parts[SEGS * ST :]
-    factor = jnp.concatenate(masks, axis=0) / (smooth * (1.0 / (2 * WF + 1)) + 1e-06)
+    flags = jnp.concatenate([jnp.concatenate(masks, axis=0)] * KT, axis=1)
+    factor = flags / (smooth * (1.0 / (2 * WF + 1)) + 1e-06)
     return (re * factor).astype(bf16).astype(f32), (im * factor).astype(bf16).astype(f32)
+
+
+def spread(flags, g):
+    return jnp.broadcast_to(flags[:, g : g + 1], (ST, 128))
 
 
 def hour(ref):
@@ -281,7 +286,7 @@
         copies[i].wait()
     weights = (fir_ref, box_ref, dft_ref, near_ref)
     masks = [own_mask[i].astype(f32) for i in range(2)]
-    columns = [m[:, g : g + 1] for m in masks for g in range(SEG)]
+    columns = [spread(m, g) for m in masks for g in range(SEG)]
     station[0], station[1] = whiten(hour(own), columns, *[w[...] for w in weights])
 
     @pl.when(collects)
@@ -310,6 +315,18 @@
 
     copies[7].wait()
 
+    @pl.when(jnp.logical_not(keeps_masks))
+    def _():
+        wait(source_mask, mthree_sem.at[1])
+
+    theirs = [source_mask[i].astype(f32) for i in range(2)]
+    columns = [spread(m, g) for m in theirs for g in range(SEG)]
+    shares = []
+    for n in range(ST):
+        count = masks[0] * theirs[0][n : n + 1] + masks[1] * theirs[1][n : n + 1]
+        count = jnp.maximum(jnp.sum(count, axis=1, keepdims=True), 1.0)
+        shares.append(jnp.broadcast_to(1.0 / count, (ST, 128)))
+
     @pl.when(collects)
     def _():
         wait(source.at[:, :, pl.ds(0, 15 * PIECE)], three_sem.at[1])
@@ -318,12 +335,6 @@
     def _():
         wait(source, three_sem.at[1])
 
-    @pl.when(jnp.logical_not(keeps_masks))
-    def _():
-        wait(source_mask, mthree_sem.at[1])
-
-    theirs = [source_mask[i].astype(f32) for i in range(2)]
-    columns = [m[:, g : g + 1] for m in theirs for g in range(SEG)]
     source_re, source_im = whiten(hour(source), columns, *[w[...] for w in weights])
     for k in range(KT):
         part = slice(128 * k, 128 * (k + 1))
@@ -345,9 +356,8 @@
     upper = parts[: ST * ST]
     lagged = upper[:, :LAGS] + upper[:, LAGS:] + parts[ST * ST :, :LAGS]
     for n in range(ST):
-        count = masks[0] * theirs[0][n : n + 1] + masks[1] * theirs[1][n : n + 1]
-        count = jnp.maximum(jnp.sum(count, axis=1, keepdims=True), 1.0)
-        out_ref[n] = lagged[ST * n : ST * (n + 1)] / count
+        share = jnp.concatenate([shares[n]] * (LAGS // 128), axis=1)
+        out_ref[n] = lagged[ST * n : ST * (n + 1)] * share
 
     @pl.when(collects)
     def _():

time: 25.9 us -> 25.9 us (level)
  no operation moved by 1% of the time
where the time goes in v9:
time: 25.9 us; the launch traced here: 25.8 us
  Pallas kernels  25.2 us (97%)
  local copies, waits for them, and re-layouts  0.63 us (2%)
    pallas_call x1, Pallas kernels, shards(): pl.pallas_call(kernel, out_shape=jax.ShapeDtypeStruct((ST, ST, LAGS), f32...  25.2 us
    unnamed x1, local copies, waits for them, and re-layouts  0.63 us

profile of v9, /device:TPU:1, one launch (start us, length us, event | category | flops | bytes accessed | tf_op | source)
XLA Modules:
  0.0 25.8 jit_solution(7704939348893453973)
XLA Ops:
  0.0 25.2 %shard_map.82 = f32[8,8,256]{2,1,0:T(8,128)S(1)} custom-call(bf16[8,4096]{1,0:T(8,128)(2,1)} %raw_hbm.1, s32[4,8]{1,0:T(4,128)} %bitcast.1, s32[128]{0:T(128)} %order_hbm.1, bf16[384,256]{1,0:T(8,128)(2,1)} %constant.10.clone.fir_hbm, bf16[512,256]{1,0:T(8,128)(2,1)} %constant.11.clone.box_hbm, bf16[1024,768]{1,0:T(8,128)(2,1)} %constant.12.clone.dft_hbm, ...), custom_call_target="tpu_custom_call" | custom-call | tf_op jit(solution)/shard_map/pallas_call | solution.py:388
  25.2 0.6 %copy.10 = f32[8,8,256]{2,1,0:T(8,128)} copy(f32[8,8,256]{2,1,0:T(8,128)S(1)} %shard_map.82) | data formatting | bytes 131072
